TPU v7x, 32 devices: a whole 2x2x4 slice. The times are simulated.
32 devices in a mesh: groups: 2 (over x), date: 16 (over z, y, core).
Axes of the slice: x: 2, y: 2, z: 4, core: 2. Of those that a mesh axis runs over, the one named last changes fastest.
Arguments:
- secondary_complex_slabs: bfloat16 [32, 2, 32, 256], P(('groups', 'date')), parts along dimension 0, may hold values from -6 to 6
- reference_complex_slab: bfloat16 [2, 256, 64], P(None, ('groups', 'date')), parts along dimension 1, may hold values from -6 to 6
- elevation_tiles: float32 [64, 8, 256], P(('groups', 'date')), parts along dimension 0, may hold values from -6 to 6
- baseline: float32 [32, 2], P(('groups', 'date')), parts along dimension 0, may hold values from -2 to 2
- block_terrain_tile: int32 [256, 1], P('groups'), parts along dimension 0, may hold values from 0 to 31
- block_first_row: int32 [256], P('groups'), parts along dimension 0, may hold values from 0 to 3
- block_first_column: int32 [256], P('groups'), parts along dimension 0, may hold values from 0 to 239
- block_fraction_weights: int32 [256, 2], P('groups'), parts along dimension 0, may hold values from 0 to 15
Outputs:
- filtered: bfloat16 [32, 2, 32, 256], P(('groups', 'date')), parts along dimension 0
There are 2 independent parts, one for each index of `groups`. A program takes and returns all parts, laid end to end along the dimension named above; each array names one. Nothing has to cross between parts.
Inputs may be any that keep to these rules, and one draw needn't show every extreme that they name: `block_terrain_tile`: every tile is named by at least one block.
All inputs are finite; a program needn't handle non-finite values.
Results may differ from a plain program's by a relative error of at most 0.0074.
Values may be sent and summed in bfloat16 or wider, within the bound.
A program may use at most 64 MiB of HBM per device.

v0:
```python
import math

import jax
import jax.numpy as jnp
from jax import lax
from jax.sharding import PartitionSpec as P

PATCH_SIZE = 64
BLOCK_LINES = 4
BLOCK_SAMPLES = 16


def dft_tables():
    series = jnp.arange(PATCH_SIZE, dtype=jnp.int32)
    angle = (series[:, None] * series[None, :] % PATCH_SIZE).astype(jnp.float32) * (
        2.0 * math.pi / PATCH_SIZE
    )
    cosine = jnp.cos(angle).astype(jnp.bfloat16)
    sine = jnp.sin(angle).astype(jnp.bfloat16)
    forward = jnp.concatenate(
        [jnp.concatenate([cosine, -sine], axis=1), jnp.concatenate([sine, cosine], axis=1)], axis=0
    )
    inverse = jnp.concatenate(
        [jnp.concatenate([cosine, sine], axis=1), jnp.concatenate([-sine, cosine], axis=1)], axis=0
    )
    taper = jnp.sin(math.pi * (series.astype(jnp.float32) + 0.5) / PATCH_SIZE) ** 2
    return (cosine, sine, forward, inverse, taper)


def block_terrain_heights(
    elevation_tiles, terrain_tile_index, block_first_row, block_first_column, block_fraction_weights
):
    tile_rows = elevation_tiles.shape[1]
    tile_cols = elevation_tiles.shape[2]
    flattened = elevation_tiles.reshape(-1)
    line_offset = jnp.arange(BLOCK_LINES + 1, dtype=jnp.int32)
    sample_offset = jnp.arange(BLOCK_SAMPLES + 1, dtype=jnp.int32)
    base_index = (
        terrain_tile_index * (tile_rows * tile_cols)
        + block_first_row * tile_cols
        + block_first_column
    )
    positions = (
        base_index[:, None, None]
        + line_offset[None, :, None] * tile_cols
        + sample_offset[None, None, :]
    )
    windows = jnp.take(flattened, positions, axis=0)
    weights = block_fraction_weights.astype(jnp.float32) / 16.0
    down_frac = weights[:, 0][:, None, None]
    right_frac = weights[:, 1][:, None, None]
    upper_row = (1.0 - right_frac) * windows[:, :-1, :-1] + right_frac * windows[:, :-1, 1:]
    lower_row = (1.0 - right_frac) * windows[:, 1:, :-1] + right_frac * windows[:, 1:, 1:]
    return (1.0 - down_frac) * upper_row + down_frac * lower_row


def to_image(block_entries, row_count, col_count):
    shaped = block_entries.reshape(
        row_count // BLOCK_LINES, col_count // BLOCK_SAMPLES, BLOCK_LINES, BLOCK_SAMPLES
    )
    return shaped.transpose(0, 2, 1, 3).reshape(row_count, col_count)


def interfere(date_slab, coeffs, reference_field, heights):
    col_count = heights.shape[1]
    across = (jnp.arange(col_count, dtype=jnp.float32) + 0.5) / col_count - 0.5
    phase = (coeffs[0] + coeffs[1] * across)[None, :] * heights
    sec_real = date_slab[0].astype(jnp.float32)
    sec_imag = date_slab[1].astype(jnp.float32)
    ref_real = reference_field[0].astype(jnp.float32)
    ref_imag = reference_field[1].astype(jnp.float32)
    cross_real = sec_real * ref_real + sec_imag * ref_imag
    cross_imag = sec_imag * ref_real - sec_real * ref_imag
    cosine = jnp.cos(phase)
    sine = jnp.sin(phase)
    real_part = (cross_real * cosine + cross_imag * sine).astype(jnp.bfloat16)
    imag_part = (cross_imag * cosine - cross_real * sine).astype(jnp.bfloat16)
    return (real_part, imag_part)


def goldstein(real_part, imag_part):
    row_count, col_count = real_part.shape
    half_size = PATCH_SIZE // 2
    cosine, sine, forward, inverse, taper = dft_tables()
    col_patches = col_count // half_size + 1
    row_patches = row_count // half_size + 1

    def split_cols(field):
        padded = jnp.pad(field, half_size)
        block_entries = padded.reshape(padded.shape[0], col_patches + 1, half_size)
        return jnp.concatenate([block_entries[:, :-1], block_entries[:, 1:]], axis=2)

    joined = jnp.concatenate([split_cols(real_part), split_cols(imag_part)], axis=2)
    patches = jnp.stack(
        [
            joined[half_size * number : half_size * number + PATCH_SIZE]
            for number in range(row_patches)
        ]
    )
    colspec = jnp.einsum(
        "piqc,cd->piqd", patches, forward, preferred_element_type=jnp.float32
    ).astype(jnp.bfloat16)
    swapped = jnp.concatenate([colspec[..., PATCH_SIZE:], -colspec[..., :PATCH_SIZE]], axis=3)
    spectrum = jnp.einsum(
        "ki,piqc->pkqc", cosine, colspec, preferred_element_type=jnp.float32
    ) + jnp.einsum("ki,piqc->pkqc", sine, swapped, preferred_element_type=jnp.float32)
    energy = spectrum[..., :PATCH_SIZE] ** 2 + spectrum[..., PATCH_SIZE:] ** 2
    row_smooth = energy + jnp.roll(energy, 1, axis=1) + jnp.roll(energy, -1, axis=1)
    smooth = (row_smooth + jnp.roll(row_smooth, 1, axis=3) + jnp.roll(row_smooth, -1, axis=3)) / 9.0
    average = jnp.mean(smooth, axis=(1, 3), keepdims=True)
    response = jnp.sqrt((smooth + 0.1 * average) / (average + 1e-06))
    weighted = (spectrum * jnp.concatenate([response, response], axis=3)).astype(jnp.bfloat16)
    turned = jnp.concatenate([weighted[..., PATCH_SIZE:], -weighted[..., :PATCH_SIZE]], axis=3)
    rowback = (
        jnp.einsum("ki,piqc->pkqc", cosine, weighted, preferred_element_type=jnp.float32)
        - jnp.einsum("ki,piqc->pkqc", sine, turned, preferred_element_type=jnp.float32)
    ).astype(jnp.bfloat16)
    patch_out = jnp.einsum("pkqc,cd->pkqd", rowback, inverse, preferred_element_type=jnp.float32)
    col_taper = jnp.concatenate([taper, taper])
    patch_out = (
        patch_out
        * taper[None, :, None, None]
        * col_taper[None, None, None, :]
        / float(PATCH_SIZE * PATCH_SIZE)
    )
    stacked = patch_out[1:, :half_size] + patch_out[:-1, half_size:]
    stacked = stacked.reshape(row_count, col_patches, 2, 2, half_size)
    merged = stacked[:, 1:, :, 0] + stacked[:, :-1, :, 1]
    return merged.transpose(2, 0, 1, 3).reshape(2, row_count, col_count).astype(jnp.bfloat16)


def per_device(
    secondary_complex_slabs,
    reference_complex_slab,
    elevation_tiles,
    baseline,
    block_terrain_tile,
    block_first_row,
    block_first_column,
    block_fraction_weights,
):
    row_count = secondary_complex_slabs.shape[2]
    col_count = secondary_complex_slabs.shape[3]
    each_terrain_tile = lax.all_gather(elevation_tiles, "date", axis=0, tiled=True)
    block_entries = block_terrain_heights(
        each_terrain_tile,
        block_terrain_tile[:, 0],
        block_first_row,
        block_first_column,
        block_fraction_weights,
    )
    heights = to_image(block_entries, row_count, col_count)
    gathered = lax.all_gather(reference_complex_slab, "date", axis=1, tiled=True)
    reference_field = gathered.reshape(2, row_count, col_count)

    def one_date(operands):
        date_slab, coeffs = operands
        real_part, imag_part = interfere(date_slab, coeffs, reference_field, heights)
        return goldstein(real_part, imag_part)

    return lax.map(one_date, (secondary_complex_slabs, baseline))


def solution(mesh):
    return jax.shard_map(
        per_device,
        mesh=mesh,
        in_specs=(
            P(("groups", "date"), None, None, None),
            P(None, ("groups", "date"), None),
            P(("groups", "date"), None, None),
            P(("groups", "date"), None),
            P("groups", None),
            P("groups"),
            P("groups"),
            P("groups", None),
        ),
        out_specs=P(("groups", "date"), None, None, None),
        check_vma=False,
    )
```

profile of v0, /device:TPU:1, one launch (start us, length us, event | category | flops | bytes accessed | tf_op | source)
XLA Modules:
  0.0 114.2 jit_solution(10767939588490026842)
XLA Ops:
  0.0 0.7 fusion.59
  0.8 0.6 copy-done
  1.9 0.7 copy-done.3
  2.6 23.7 %all_gather.7 = f32[32,8,256]{2,1,0:T(8,128)S(1)} all-gather(f32[2,8,256]{2,1,0:T(8,128)S(1)} %copy-done.3), channel_id=1, replica_groups=mesh['groups'=2,'date'=16] {'date'}, dimensions={0}, use_global_device_ids=true | all-gather | bytes 278528 | tf_op jit(solution)/shard_map/all_gather | solution.py:144
  26.4 56.2 %gather_fusion = f32[10880]{0:T(1024)S(1)} fusion(f32[65536]{0:T(1024)S(1)} %bitcast.98, s32[11264]{0:T(1024)S(1)} %pad_clamp_fusion), kind=kCustom, calls=%fused_computation | custom fusion | bytes 130560 | tf_op jit(solution)/shard_map/jit(_take)/gather | solution.py:48
  83.0 0.5 copy-done.1
  83.5 0.7 copy-done.6
  84.7 0.5 copy-done.5
  85.2 0.6 fusion.87
  85.8 1.3 %multiply_add_fusion.1 = f32[256]{0:T(256)S(1)} fusion(f32[]{:T(128)} %bitcast.3, f32[]{:T(128)} %bitcast.2), kind=kLoop, calls=%fused_computation.100 | loop fusion | flops 1280 | bytes 1032 | tf_op jit(solution)/shard_map/while/body/eval_jaxpr/add | solution.py:67
  87.1 17.6 %all_gather.6 = bf16[2,128,64]{2,1,0:T(8,128)(2,1)S(1)} all-gather(bf16[2,8,64]{2,1,0:T(8,128)(2,1)S(1)} %copy-done.4), channel_id=1, replica_groups=mesh['groups'=2,'date'=16] {'date'}, dimensions={1}, use_global_device_ids=true | all-gather | bytes 34816 | tf_op jit(solution)/shard_map/all_gather | solution.py:153
  104.9 0.7 copy-done.2
  107.0 0.3 pad_maximum_fusion
  107.6 0.3 convolution_convert_fusion
  108.1 0.3 fusion.51
  108.4 0.4 fusion.2
  109.2 0.4 fusion.6
  110.0 0.5 fusion.76
  111.2 0.3 fusion.53
  111.6 0.5 fusion.1
  112.1 0.5 reshape.164
  112.6 0.5 fusion.78
  113.1 0.3 fusion.23
  113.6 0.6 copy.43
  (56 shorter events, 5.3 us)
Async XLA Ops:
  0.8 0.6 copy-start
  1.9 0.7 copy-start.3
  82.8 0.7 copy-start.1
  83.5 0.7 copy-start.6
  84.5 0.7 copy-start.5
  85.8 1.3 %copy-start.4 = (bf16[2,8,64]{2,1,0:T(8,128)(2,1)S(1)}, bf16[2,8,64]{2,1,0:T(8,128)(2,1)}, u32[]{:S(2)}) copy-start(bf16[2,8,64]{2,1,0:T(8,128)(2,1)} %param.9) | copy-start | bytes 6148
  104.8 0.8 copy-start.2
where the time goes:
time: 115 us; the launch traced here: 114 us
  local copies, waits for them, and re-layouts  65.4 us (57%)
  blocking collectives  41.3 us (36%)
  other arithmetic  5.4 us (5%)
  matrix products  1.87 us (2%)
    gather x3, local copies, waits for them, and re-layouts, block_terrain_heights(): windows = jnp.take(flattened, positions, axis=0)  56.6 us
    all_gather x1, blocking collectives, per_device(): lax.all_gather(elevation_tiles, 'date', axis=0, tiled=True)  23.7 us
    all_gather x1, blocking collectives, per_device(): lax.all_gather(reference_complex_slab, 'date', axis=1, tiled=True)  17.6 us
    unnamed x21, local copies, waits for them, and re-layouts  4.73 us

commit v1 on v0

v1 whole, which is shorter than its diff:
```python
import functools
import math

import jax
import jax.numpy as jnp
import ml_dtypes
import numpy as np
from jax import lax
from jax.experimental import pallas as pl
from jax.experimental.pallas import tpu as pltpu
from jax.sharding import PartitionSpec as P

PATCH_SIZE = 64
HALF = PATCH_SIZE // 2
BLOCK_LINES = 4
BLOCK_SAMPLES = 16
LANES = 128
SUBLANES = 8
SPAN = LANES // HALF + 1
SPAN_LANES = -(-SPAN * PATCH_SIZE // LANES) * LANES
GROUP_STEP = (SPAN - 1) * PATCH_SIZE


@functools.lru_cache(maxsize=None)
def tables():
    series = np.arange(PATCH_SIZE)
    angle = (series[:, None] * series[None, :] % PATCH_SIZE) * (2.0 * math.pi / PATCH_SIZE)
    cosine, sine = np.cos(angle), np.sin(angle)
    taper = np.sin(math.pi * (series + 0.5) / PATCH_SIZE) ** 2 / (PATCH_SIZE * PATCH_SIZE)
    into = np.zeros((2, LANES, SPAN_LANES))
    back = np.zeros((2, SPAN_LANES, 2, LANES))
    for m in range(LANES):
        block, j = divmod(m, HALF)
        for half, (q, n) in enumerate(((block, HALF + j), (block + 1, j))):
            lanes = slice(q * PATCH_SIZE, (q + 1) * PATCH_SIZE)
            into[0, m, lanes] = cosine[n]
            into[1, m, lanes] = sine[n]
            back[0, lanes, half, m] = cosine[:, n]
            back[1, lanes, half, m] = -sine[:, n]
    into = into.reshape(2 * LANES, SPAN_LANES)
    back = back.reshape(2 * SPAN_LANES, 2 * LANES)
    c, s = cosine[:, :HALF], sine[:, :HALF]
    down = np.block([[c, s], [-s, c]])
    c, s = cosine[:HALF], sine[:HALF]
    up = np.block([[c, -s], [s, c]])
    weights = np.stack([np.tile(taper[HALF:], LANES // HALF), np.tile(taper[:HALF], LANES // HALF)])
    placed = tuple(m.astype(np.float32).astype(ml_dtypes.bfloat16) for m in (into, down, up, back))
    return placed + (weights.astype(np.float32),)


def kernel(
    n,
    elev, ref_in, sec, base, first_tile, first_row, first_col, frac,
    into_h, down_h, up_h, back_h, taper_h,
    out,
    tiles, refbuf, refwide, heights, secbuf, into, down, up, back, taper,
    local_sem, send_sem, recv_sem, fwd_sem,
):
    rows, cols = sec.shape[2], sec.shape[3]
    own = elev.shape[0]
    me = lax.axis_index("date")
    partner = me + 1 - 2 * (me % 2)
    peers = [(me + 2 * k) % n for k in range(1, n // 2)]
    sources = [(me + n - 2 * k) % n for k in range(1, n // 2)]
    barrier = pltpu.get_barrier_semaphore()
    for peer in peers + [partner]:
        pl.semaphore_signal(
            barrier, inc=1, device_id={"date": peer}, device_id_type=pl.DeviceIdType.MESH
        )

    def slot(device):
        return tiles.at[pl.ds(device * own, own)]

    local = [
        pltpu.make_async_copy(ref_in, refbuf.at[me], local_sem.at[0]),
        pltpu.make_async_copy(elev, slot(me), local_sem.at[1]),
        pltpu.make_async_copy(sec, secbuf, local_sem.at[2]),
        pltpu.make_async_copy(into_h, into, local_sem.at[3]),
        pltpu.make_async_copy(down_h, down, local_sem.at[4]),
        pltpu.make_async_copy(up_h, up, local_sem.at[5]),
        pltpu.make_async_copy(back_h, back, local_sem.at[6]),
        pltpu.make_async_copy(taper_h, taper, local_sem.at[7]),
    ]
    for copy in local:
        copy.start()

    def remote(src, dst, sends, number, kind, source, device):
        return pltpu.make_async_remote_copy(
            src_ref=src,
            dst_ref=dst,
            send_sem=sends.at[kind, number],
            recv_sem=recv_sem.at[kind, source],
            device_id={"date": device},
            device_id_type=pl.DeviceIdType.MESH,
        )

    pl.semaphore_wait(barrier, n // 2)
    sent = []
    for number, peer in enumerate(peers + [partner]):
        sent.append(remote(ref_in, refbuf.at[me], send_sem, number, 0, me, peer))
        sent[-1].start()
    for number, peer in enumerate(peers + [partner]):
        sent.append(remote(elev, slot(me), send_sem, number, 1, me, peer))
        sent[-1].start()
    for kind in range(2):
        for number, source in enumerate(sources):
            where = refbuf.at[source] if kind == 0 else slot(source)
            copy = remote(where, where, fwd_sem, number, kind, source, partner)
            copy.wait_recv()
            copy.start()
            sent.append(copy)
    others = [partner] + [source + 1 - 2 * (source % 2) for source in sources]
    for source in others:
        remote(refbuf.at[source], refbuf.at[source], send_sem, 0, 0, source, partner).wait_recv()
    local[0].wait()

    line = refbuf.shape[3]
    per_row = cols // line
    field = []
    for part in range(2):
        refwide[part] = refbuf[:, part].astype(jnp.float32).reshape(rows * per_row, line)
        field.append(
            jnp.concatenate(
                [refwide[part, pl.ds(m, rows, stride=per_row), :] for m in range(per_row)], axis=1
            )
        )
    for copy in local[2:]:
        copy.wait()
    lane_row = lax.broadcasted_iota(jnp.int32, (1, cols), 1).astype(jnp.float32)
    across = (lane_row + 0.5) / cols - 0.5

    for source in others:
        remote(slot(source), slot(source), send_sem, 0, 1, source, partner).wait_recv()
    local[1].wait()

    lane = lax.broadcasted_iota(jnp.int32, (SUBLANES, LANES), 1)
    sublane = lax.broadcasted_iota(jnp.int32, (SUBLANES, LANES), 0)
    grid_cols = cols // BLOCK_SAMPLES
    per_group = LANES // BLOCK_SAMPLES
    bands = SUBLANES // BLOCK_LINES

    def eight_rows(step, carry):
        for group in range(cols // LANES):
            total = jnp.zeros((SUBLANES, LANES), jnp.float32)
            for band in range(bands):
                for place in range(per_group):
                    b = (step * bands + band) * grid_cols + group * per_group + place
                    tile, col = first_tile[b], first_col[b]
                    fy = frac[0, b].astype(jnp.float32) * (1.0 / 16.0)
                    fx = frac[1, b].astype(jnp.float32) * (1.0 / 16.0)
                    near = tiles[tile, :, 0:LANES]
                    for other in range(1, cols // LANES):
                        far = tiles[tile, :, other * LANES : (other + 1) * LANES]
                        near = jnp.where(lane + (other - 1) * LANES >= col, near, far)
                    move = band * BLOCK_LINES + SUBLANES - first_row[b]
                    upper = pltpu.roll(near, lax.rem(move, SUBLANES), 0)
                    lower = pltpu.roll(near, lax.rem(move - 1, SUBLANES), 0)
                    mixed = upper + fy * (lower - upper)
                    shift = place * BLOCK_SAMPLES + cols - col
                    left = pltpu.roll(mixed, lax.rem(shift, LANES), 1)
                    right = pltpu.roll(mixed, lax.rem(shift - 1, LANES), 1)
                    value = left + fx * (right - left)
                    inside = (lane // BLOCK_SAMPLES == place) & (sublane // BLOCK_LINES == band)
                    total = jnp.where(inside, value, total)
            heights[
                pl.ds(pl.multiple_of(step * SUBLANES, SUBLANES), SUBLANES),
                group * LANES : (group + 1) * LANES,
            ] = total
        return carry

    lax.fori_loop(0, rows // SUBLANES, eight_rows, 0)

    groups = cols // LANES
    lanes64 = lax.broadcasted_iota(jnp.int32, (PATCH_SIZE, LANES), 1) % PATCH_SIZE
    first, last = lanes64 == 0, lanes64 == PATCH_SIZE - 1
    same_patch = (
        lax.broadcasted_iota(jnp.int32, (2 * LANES, LANES), 0) % LANES // PATCH_SIZE
        == lax.broadcasted_iota(jnp.int32, (2 * LANES, LANES), 1) // PATCH_SIZE
    )
    ones = jnp.where(same_patch, 1.0, 0.0).astype(jnp.bfloat16)

    def dot(a, b):
        return jnp.dot(a, b, preferred_element_type=jnp.float32)

    for date in range(sec.shape[0]):
        phase = (base[date, 0] + base[date, 1] * across) * heights[...]
        sec_real = secbuf[date, 0].astype(jnp.float32)
        sec_imag = secbuf[date, 1].astype(jnp.float32)
        cross_real = sec_real * field[0] + sec_imag * field[1]
        cross_imag = sec_imag * field[0] - sec_real * field[1]
        cosine, sine = jnp.cos(phase), jnp.sin(phase)
        real = (cross_real * cosine + cross_imag * sine).astype(jnp.bfloat16)
        imag = (cross_imag * cosine - cross_real * sine).astype(jnp.bfloat16)
        left = []
        for g in range(groups):
            re, im = (x[:, g * LANES : (g + 1) * LANES] for x in (real, imag))
            left.append(jnp.concatenate([re, im], axis=1))
            left.append(jnp.concatenate([im, -re], axis=1))
        product = dot(jnp.concatenate(left, axis=0), into[...])
        pieces = [None] * ((groups * GROUP_STEP + SPAN_LANES - GROUP_STEP) // LANES)
        for g in range(groups):
            for k in range(SPAN_LANES // LANES):
                term = product[
                    2 * rows * g : 2 * rows * (g + 1), k * LANES : (k + 1) * LANES
                ]
                at = g * GROUP_STEP // LANES + k
                pieces[at] = term if pieces[at] is None else pieces[at] + term
        colspec = jnp.concatenate(pieces, axis=1).astype(jnp.bfloat16)
        spectrum = dot(down[...], colspec)
        parts = []
        sums = []
        for k in range(len(pieces)):
            here = spectrum[:, k * LANES : (k + 1) * LANES]
            re, im = here[:PATCH_SIZE], here[PATCH_SIZE:]
            energy = re * re + im * im
            total = energy[0:SUBLANES]
            for r in range(1, PATCH_SIZE // SUBLANES):
                total = total + energy[r * SUBLANES : (r + 1) * SUBLANES]
            sums.append(total)
            parts.append((re, im, energy))
        total = jnp.concatenate(sums, axis=0)
        high = total.astype(jnp.bfloat16)
        low = (total - high.astype(jnp.float32)).astype(jnp.bfloat16)
        means = dot(jnp.concatenate([high, low], axis=1), ones)
        weighted = []
        for k, (re, im, energy) in enumerate(parts):
            mean = jnp.sum(means[k * SUBLANES : (k + 1) * SUBLANES], axis=0, keepdims=True)
            mean = mean / float(PATCH_SIZE * PATCH_SIZE)
            tall = energy + pltpu.roll(energy, 1, 0) + pltpu.roll(energy, PATCH_SIZE - 1, 0)
            before = jnp.where(
                first, pltpu.roll(tall, LANES + 1 - PATCH_SIZE, 1), pltpu.roll(tall, 1, 1)
            )
            after = jnp.where(
                last, pltpu.roll(tall, PATCH_SIZE - 1, 1), pltpu.roll(tall, LANES - 1, 1)
            )
            smooth = (tall + before + after) * (1.0 / 9.0)
            response = jnp.sqrt((smooth + 0.1 * mean) * (1.0 / (mean + 1e-06)))
            weighted.append(
                jnp.concatenate([re * response, im * response], axis=0).astype(jnp.bfloat16)
            )
        rowback = dot(up[...], jnp.concatenate(weighted, axis=1)).astype(jnp.bfloat16)
        left = []
        for g in range(groups):
            here = rowback[:, g * GROUP_STEP : g * GROUP_STEP + SPAN_LANES]
            re, im = here[:rows], here[rows:]
            left.append(jnp.concatenate([re, im], axis=1))
            left.append(jnp.concatenate([im, -re], axis=1))
        product = dot(jnp.concatenate(left, axis=0), back[...])
        merged = product[:, :LANES] * taper[0:1, :] + product[:, LANES:] * taper[1:2, :]
        merged = merged.astype(jnp.bfloat16)
        for g in range(groups):
            for part in range(2):
                begin = (2 * g + part) * rows
                out[date, part, :, g * LANES : (g + 1) * LANES] = merged[begin : begin + rows]

    for copy in sent:
        copy.wait_send()


def per_device(
    n,
    secondary_complex_slabs,
    reference_complex_slab,
    elevation_tiles,
    baseline,
    block_terrain_tile,
    block_first_row,
    block_first_column,
    block_fraction_weights,
):
    dates, _, rows, cols = secondary_complex_slabs.shape
    assert rows == HALF and elevation_tiles.shape[1:] == (SUBLANES, cols)
    lines, line = reference_complex_slab.shape[1:]
    constants = [jnp.asarray(table) for table in tables()]
    anywhere = pl.BlockSpec(memory_space=pl.ANY)
    scalars = pl.BlockSpec(memory_space=pltpu.SMEM)
    return pl.pallas_call(
        functools.partial(kernel, n),
        out_shape=jax.ShapeDtypeStruct(secondary_complex_slabs.shape, jnp.bfloat16),
        in_specs=[anywhere] * 3 + [scalars] * 5 + [anywhere] * 5,
        out_specs=pl.BlockSpec(memory_space=pltpu.VMEM),
        scratch_shapes=[
            pltpu.VMEM((n * elevation_tiles.shape[0],) + elevation_tiles.shape[1:], jnp.float32),
            pltpu.VMEM((n, 2, lines, line), jnp.bfloat16),
            pltpu.VMEM((2, n * lines, line), jnp.float32),
            pltpu.VMEM((rows, cols), jnp.float32),
            pltpu.VMEM(secondary_complex_slabs.shape, jnp.bfloat16),
        ]
        + [pltpu.VMEM(table.shape, table.dtype) for table in constants]
        + [
            pltpu.SemaphoreType.DMA((8,)),
            pltpu.SemaphoreType.DMA((2, n // 2)),
            pltpu.SemaphoreType.DMA((2, n)),
            pltpu.SemaphoreType.DMA((2, n // 2)),
        ],
        compiler_params=pltpu.CompilerParams(collective_id=0, has_side_effects=True),
    )(
        elevation_tiles,
        reference_complex_slab,
        secondary_complex_slabs,
        baseline,
        block_terrain_tile.reshape(-1),
        block_first_row,
        block_first_column,
        block_fraction_weights.T,
        *constants,
    )


def solution(mesh):
    return jax.shard_map(
        functools.partial(per_device, mesh.shape["date"]),
        mesh=mesh,
        in_specs=(
            P(("groups", "date"), None, None, None),
            P(None, ("groups", "date"), None),
            P(("groups", "date"), None, None),
            P(("groups", "date"), None),
            P("groups", None),
            P("groups"),
            P("groups"),
            P("groups", None),
        ),
        out_specs=P(("groups", "date"), None, None, None),
        check_vma=False,
    )
```

time: 115 us -> 17.4 us (0.15)
  local copies, waits for them, and re-layouts: 65.4 us -> 1.38 us
  blocking collectives: 41.3 us -> 0 us
  Pallas kernels: 0 us -> 15.8 us
  other arithmetic: 5.4 us -> 0 us
  matrix products: 1.87 us -> 0 us
    gather x3 -> x0, local copies, waits for them, and re-layouts: 56.6 us -> none  [block_terrain_heights(): windows = jnp.take(flattened, positions, axis=0)]
    all_gather x2 -> x0, blocking collectives: 41.3 us -> none  [the longest x1 23.7 us: per_device(): lax.all_gather(elevation_tiles, 'date', axis=0, tiled=True)]
    pallas_call x0 -> x1, Pallas kernels: none -> 15.8 us  [per_device(): pl.pallas_call(functools.partial(kernel, n), out_shape=jax.ShapeDtypeStru...]
    unnamed x21 -> x1, local copies, waits for them, and re-layouts: 4.73 us -> 1.38 us
    add x7 -> x0, other arithmetic: 2.69 us -> none  [the longest x1 1.3 us: interfere(): phase = (coeffs[0] + coeffs[1] * across)[None, :] * heights]
    dot_general x5 -> x0, matrix products: 1.87 us -> none  [the longest x1 0.46 us: goldstein(): jnp.einsum('pkqc,cd->pkqd', rowback, inverse, preferred_element_type=jnp....]
    slice x8 -> x0, local copies, waits for them, and re-layouts: 1.71 us -> none  [the longest x1 0.61 us: interfere(): phase = (coeffs[0] + coeffs[1] * across)[None, :] * heights]
where the time goes in v1:
time: 17.4 us; the launch traced here: 17.2 us
  Pallas kernels  15.8 us (91%)
  local copies, waits for them, and re-layouts  1.38 us (8%)
    pallas_call x1, Pallas kernels, per_device(): pl.pallas_call(functools.partial(kernel, n), out_shape=jax.ShapeDtypeStru...  15.8 us
    unnamed x1, local copies, waits for them, and re-layouts  1.38 us

profile of v1, /device:TPU:1, one launch (start us, length us, event | category | flops | bytes accessed | tf_op | source)
XLA Modules:
  0.0 17.2 jit_solution(2245506769337934871)
XLA Ops:
  0.0 15.8 %shard_map.127 = bf16[1,2,32,256]{3,2,1,0:T(8,128)(2,1)} custom-call(f32[2,8,256]{2,1,0:T(8,128)} %elev.1, bf16[2,8,64]{2,1,0:T(8,128)(2,1)} %ref_in.1, bf16[1,2,32,256]{3,2,1,0:T(8,128)(2,1)} %sec.1, f32[1,2]{1,0:T(1,128)} %base.1, s32[128]{0:T(128)} %bitcast.3, s32[128]{0:T(128)} %first_row.1, s32[128]{0:T(128)} %first_col.1, s32[2,128]{1,0:T(2,128)} %bitcast.2, ...), custom_call_target="tpu_custom_call" | custom-call | tf_op jit(solution)/shard_map/pallas_call | solution.py:277
  15.8 1.4 %copy.15 = bf16[1,2,32,256]{3,2,1,0:T(8,128)(2,1)} copy(bf16[1,2,32,256]{3,2,1,0:T(8,128)(2,1)} %shard_map.127) | data formatting | bytes 65536

commit v2 on v1

--- a/solution.py
+++ b/solution.py
@@ -48,20 +48,31 @@
     return placed + (weights.astype(np.float32),)
 
 
+def flipped(index, bits):
+    result = index
+    bit = 1
+    while bit <= bits:
+        if bits & bit:
+            result = result + bit - 2 * bit * (index // bit % 2)
+        bit *= 2
+    return result
+
+
 def kernel(
     n,
-    elev, ref_in, sec, base, first_tile, first_row, first_col, frac,
+    elev, ref_in, sec, base_h, tile_h, row_h, col_h, frac_h,
     into_h, down_h, up_h, back_h, taper_h,
     out,
     tiles, refbuf, refwide, heights, secbuf, into, down, up, back, taper,
+    base, first_tile, first_row, first_col, frac,
     local_sem, send_sem, recv_sem, fwd_sem,
 ):
     rows, cols = sec.shape[2], sec.shape[3]
     own = elev.shape[0]
     me = lax.axis_index("date")
-    partner = me + 1 - 2 * (me % 2)
-    peers = [(me + 2 * k) % n for k in range(1, n // 2)]
-    sources = [(me + n - 2 * k) % n for k in range(1, n // 2)]
+    partner = flipped(me, 1)
+    peers = [flipped(me, 2 * k) for k in reversed(range(1, n // 2))]
+    sources = peers[::-1]
     barrier = pltpu.get_barrier_semaphore()
     for peer in peers + [partner]:
         pl.semaphore_signal(
@@ -80,6 +91,11 @@
         pltpu.make_async_copy(up_h, up, local_sem.at[5]),
         pltpu.make_async_copy(back_h, back, local_sem.at[6]),
         pltpu.make_async_copy(taper_h, taper, local_sem.at[7]),
+        pltpu.make_async_copy(base_h, base, local_sem.at[8]),
+        pltpu.make_async_copy(tile_h, first_tile, local_sem.at[9]),
+        pltpu.make_async_copy(row_h, first_row, local_sem.at[10]),
+        pltpu.make_async_copy(col_h, first_col, local_sem.at[11]),
+        pltpu.make_async_copy(frac_h, frac, local_sem.at[12]),
     ]
     for copy in local:
         copy.start()
@@ -96,24 +112,63 @@
 
     pl.semaphore_wait(barrier, n // 2)
     sent = []
-    for number, peer in enumerate(peers + [partner]):
-        sent.append(remote(ref_in, refbuf.at[me], send_sem, number, 0, me, peer))
-        sent[-1].start()
-    for number, peer in enumerate(peers + [partner]):
-        sent.append(remote(elev, slot(me), send_sem, number, 1, me, peer))
-        sent[-1].start()
-    for kind in range(2):
+    for kind in (1, 0):
+        for number, peer in enumerate(peers + [partner]):
+            src, dst = (elev, slot(me)) if kind else (ref_in, refbuf.at[me])
+            sent.append(remote(src, dst, send_sem, number, kind, me, peer))
+            sent[-1].start()
+    for kind in (1, 0):
         for number, source in enumerate(sources):
-            where = refbuf.at[source] if kind == 0 else slot(source)
+            where = slot(source) if kind else refbuf.at[source]
             copy = remote(where, where, fwd_sem, number, kind, source, partner)
             copy.wait_recv()
             copy.start()
             sent.append(copy)
-    others = [partner] + [source + 1 - 2 * (source % 2) for source in sources]
+    others = [partner] + [flipped(source, 1) for source in sources]
+    for copy in local:
+        copy.wait()
+    for source in others:
+        remote(slot(source), slot(source), send_sem, 0, 1, source, partner).wait_recv()
+
+    lane = lax.broadcasted_iota(jnp.int32, (SUBLANES, LANES), 1)
+    sublane = lax.broadcasted_iota(jnp.int32, (SUBLANES, LANES), 0)
+    grid_cols = cols // BLOCK_SAMPLES
+    per_group = LANES // BLOCK_SAMPLES
+    bands = SUBLANES // BLOCK_LINES
+
+    def eight_rows(step, carry):
+        for group in range(cols // LANES):
+            total = jnp.zeros((SUBLANES, LANES), jnp.float32)
+            for band in range(bands):
+                for place in range(per_group):
+                    b = (step * bands + band) * grid_cols + group * per_group + place
+                    tile, col = first_tile[b], first_col[b]
+                    fy = frac[0, b].astype(jnp.float32)
+                    fx = frac[1, b].astype(jnp.float32)
+                    near = tiles[tile, :, 0:LANES]
+                    for other in range(1, cols // LANES):
+                        far = tiles[tile, :, other * LANES : (other + 1) * LANES]
+                        near = jnp.where(lane + (other - 1) * LANES >= col, near, far)
+                    move = band * BLOCK_LINES + SUBLANES - first_row[b]
+                    upper = pltpu.roll(near, (move) & (SUBLANES - 1), 0)
+                    lower = pltpu.roll(near, (move - 1) & (SUBLANES - 1), 0)
+                    mixed = 16.0 * upper + fy * (lower - upper)
+                    shift = place * BLOCK_SAMPLES + cols - col
+                    left = pltpu.roll(mixed, (shift) & (LANES - 1), 1)
+                    right = pltpu.roll(mixed, (shift - 1) & (LANES - 1), 1)
+                    value = 16.0 * left + fx * (right - left)
+                    inside = (lane // BLOCK_SAMPLES == place) & (sublane // BLOCK_LINES == band)
+                    total = jnp.where(inside, value, total)
+            heights[
+                pl.ds(pl.multiple_of(step * SUBLANES, SUBLANES), SUBLANES),
+                group * LANES : (group + 1) * LANES,
+            ] = total * (1.0 / 256.0)
+        return carry
+
+    lax.fori_loop(0, rows // SUBLANES, eight_rows, 0)
+
     for source in others:
         remote(refbuf.at[source], refbuf.at[source], send_sem, 0, 0, source, partner).wait_recv()
-    local[0].wait()
-
     line = refbuf.shape[3]
     per_row = cols // line
     field = []
@@ -124,51 +179,8 @@
                 [refwide[part, pl.ds(m, rows, stride=per_row), :] for m in range(per_row)], axis=1
             )
         )
-    for copy in local[2:]:
-        copy.wait()
     lane_row = lax.broadcasted_iota(jnp.int32, (1, cols), 1).astype(jnp.float32)
     across = (lane_row + 0.5) / cols - 0.5
-
-    for source in others:
-        remote(slot(source), slot(source), send_sem, 0, 1, source, partner).wait_recv()
-    local[1].wait()
-
-    lane = lax.broadcasted_iota(jnp.int32, (SUBLANES, LANES), 1)
-    sublane = lax.broadcasted_iota(jnp.int32, (SUBLANES, LANES), 0)
-    grid_cols = cols // BLOCK_SAMPLES
-    per_group = LANES // BLOCK_SAMPLES
-    bands = SUBLANES // BLOCK_LINES
-
-    def eight_rows(step, carry):
-        for group in range(cols // LANES):
-            total = jnp.zeros((SUBLANES, LANES), jnp.float32)
-            for band in range(bands):
-                for place in range(per_group):
-                    b = (step * bands + band) * grid_cols + group * per_group + place
-                    tile, col = first_tile[b], first_col[b]
-                    fy = frac[0, b].astype(jnp.float32) * (1.0 / 16.0)
-                    fx = frac[1, b].astype(jnp.float32) * (1.0 / 16.0)
-                    near = tiles[tile, :, 0:LANES]
-                    for other in range(1, cols // LANES):
-                        far = tiles[tile, :, other * LANES : (other + 1) * LANES]
-                        near = jnp.where(lane + (other - 1) * LANES >= col, near, far)
-                    move = band * BLOCK_LINES + SUBLANES - first_row[b]
-                    upper = pltpu.roll(near, lax.rem(move, SUBLANES), 0)
-                    lower = pltpu.roll(near, lax.rem(move - 1, SUBLANES), 0)
-                    mixed = upper + fy * (lower - upper)
-                    shift = place * BLOCK_SAMPLES + cols - col
-                    left = pltpu.roll(mixed, lax.rem(shift, LANES), 1)
-                    right = pltpu.roll(mixed, lax.rem(shift - 1, LANES), 1)
-                    value = left + fx * (right - left)
-                    inside = (lane // BLOCK_SAMPLES == place) & (sublane // BLOCK_LINES == band)
-                    total = jnp.where(inside, value, total)
-            heights[
-                pl.ds(pl.multiple_of(step * SUBLANES, SUBLANES), SUBLANES),
-                group * LANES : (group + 1) * LANES,
-            ] = total
-        return carry
-
-    lax.fori_loop(0, rows // SUBLANES, eight_rows, 0)
 
     groups = cols // LANES
     lanes64 = lax.broadcasted_iota(jnp.int32, (PATCH_SIZE, LANES), 1) % PATCH_SIZE
@@ -273,11 +285,17 @@
     lines, line = reference_complex_slab.shape[1:]
     constants = [jnp.asarray(table) for table in tables()]
     anywhere = pl.BlockSpec(memory_space=pl.ANY)
-    scalars = pl.BlockSpec(memory_space=pltpu.SMEM)
+    scalars = (
+        baseline,
+        block_terrain_tile.reshape(-1),
+        block_first_row,
+        block_first_column,
+        block_fraction_weights.T,
+    )
     return pl.pallas_call(
         functools.partial(kernel, n),
-        out_shape=jax.ShapeDtypeStruct(secondary_complex_slabs.shape, jnp.bfloat16),
-        in_specs=[anywhere] * 3 + [scalars] * 5 + [anywhere] * 5,
+        out_shape=pltpu.VMEM(secondary_complex_slabs.shape, jnp.bfloat16),
+        in_specs=[anywhere] * 13,
         out_specs=pl.BlockSpec(memory_space=pltpu.VMEM),
         scratch_shapes=[
             pltpu.VMEM((n * elevation_tiles.shape[0],) + elevation_tiles.shape[1:], jnp.float32),
@@ -287,8 +305,9 @@
             pltpu.VMEM(secondary_complex_slabs.shape, jnp.bfloat16),
         ]
         + [pltpu.VMEM(table.shape, table.dtype) for table in constants]
+        + [pltpu.SMEM(x.shape, x.dtype) for x in scalars]
         + [
-            pltpu.SemaphoreType.DMA((8,)),
+            pltpu.SemaphoreType.DMA((13,)),
             pltpu.SemaphoreType.DMA((2, n // 2)),
             pltpu.SemaphoreType.DMA((2, n)),
             pltpu.SemaphoreType.DMA((2, n // 2)),
@@ -298,11 +317,7 @@
         elevation_tiles,
         reference_complex_slab,
         secondary_complex_slabs,
-        baseline,
-        block_terrain_tile.reshape(-1),
-        block_first_row,
-        block_first_column,
-        block_fraction_weights.T,
+        *scalars,
         *constants,
     )
 

time: 17.4 us -> 14.8 us (0.85)
  Pallas kernels: 15.8 us -> 14.1 us
  local copies, waits for them, and re-layouts: 1.38 us -> 0.62 us
    pallas_call x1, Pallas kernels: 15.8 us -> 14.1 us  [per_device(): pl.pallas_call(functools.partial(kernel, n), out_shape=pltpu.VMEM(seconda...]
    unnamed x1, local copies, waits for them, and re-layouts: 1.38 us -> 0.62 us
where the time goes in v2:
time: 14.8 us; the launch traced here: 14.7 us
  Pallas kernels  14.1 us (95%)
  local copies, waits for them, and re-layouts  0.62 us (4%)
    pallas_call x1, Pallas kernels, per_device(): pl.pallas_call(functools.partial(kernel, n), out_shape=pltpu.VMEM(seconda...  14.1 us
    unnamed x1, local copies, waits for them, and re-layouts  0.62 us

profile of v2, /device:TPU:1, one launch (start us, length us, event | category | flops | bytes accessed | tf_op | source)
XLA Modules:
  0.0 14.7 jit_solution(6537174586525658038)
XLA Ops:
  0.0 14.1 %shard_map.127 = bf16[1,2,32,256]{3,2,1,0:T(8,128)(2,1)S(1)} custom-call(f32[2,8,256]{2,1,0:T(8,128)} %elev.1, bf16[2,8,64]{2,1,0:T(8,128)(2,1)} %ref_in.1, bf16[1,2,32,256]{3,2,1,0:T(8,128)(2,1)} %sec.1, f32[1,2]{1,0:T(1,128)} %base_h.1, s32[128]{0:T(128)} %bitcast.3, s32[128]{0:T(128)} %row_h.1, s32[128]{0:T(128)} %col_h.1, s32[2,128]{1,0:T(2,128)} %bitcast.2, ...), custom_call_target="tpu_custom_call" | custom-call | tf_op jit(solution)/shard_map/pallas_call | solution.py:295
  14.1 0.6 %copy.15 = bf16[1,2,32,256]{3,2,1,0:T(8,128)(2,1)} copy(bf16[1,2,32,256]{3,2,1,0:T(8,128)(2,1)S(1)} %shard_map.127) | data formatting | bytes 65536

commit v3 on v2

--- a/solution.py
+++ b/solution.py
@@ -14,6 +14,8 @@
 HALF = PATCH_SIZE // 2
 BLOCK_LINES = 4
 BLOCK_SAMPLES = 16
+HEIGHT_REACH = 6.0
+HEIGHT_STEPS = 32767.0
 LANES = 128
 SUBLANES = 8
 SPAN = LANES // HALF + 1
@@ -63,7 +65,7 @@
     elev, ref_in, sec, base_h, tile_h, row_h, col_h, frac_h,
     into_h, down_h, up_h, back_h, taper_h,
     out,
-    tiles, refbuf, refwide, heights, secbuf, into, down, up, back, taper,
+    tiles, elevbuf, codes, refbuf, refwide, heights, secbuf, into, down, up, back, taper,
     base, first_tile, first_row, first_col, frac,
     local_sem, send_sem, recv_sem, fwd_sem,
 ):
@@ -80,11 +82,16 @@
         )
 
     def slot(device):
-        return tiles.at[pl.ds(device * own, own)]
+        return codes.at[device]
+
+    def decode(device):
+        tiles[pl.ds(device * own, own)] = (
+            codes[device].astype(jnp.int32).astype(jnp.float32).reshape(elev.shape)
+        )
 
     local = [
         pltpu.make_async_copy(ref_in, refbuf.at[me], local_sem.at[0]),
-        pltpu.make_async_copy(elev, slot(me), local_sem.at[1]),
+        pltpu.make_async_copy(elev, elevbuf, local_sem.at[1]),
         pltpu.make_async_copy(sec, secbuf, local_sem.at[2]),
         pltpu.make_async_copy(into_h, into, local_sem.at[3]),
         pltpu.make_async_copy(down_h, down, local_sem.at[4]),
@@ -97,7 +104,8 @@
         pltpu.make_async_copy(col_h, first_col, local_sem.at[11]),
         pltpu.make_async_copy(frac_h, frac, local_sem.at[12]),
     ]
-    for copy in local:
+    local[1].start()
+    for copy in local[8:] + local[:1] + local[2:8]:
         copy.start()
 
     def remote(src, dst, sends, number, kind, source, device):
@@ -110,11 +118,14 @@
             device_id_type=pl.DeviceIdType.MESH,
         )
 
+    local[1].wait()
+    scaled = jnp.round(elevbuf[...].reshape(codes.shape[1:]) * (HEIGHT_STEPS / HEIGHT_REACH))
+    codes[me] = scaled.astype(jnp.int32).astype(jnp.int16)
     pl.semaphore_wait(barrier, n // 2)
     sent = []
     for kind in (1, 0):
         for number, peer in enumerate(peers + [partner]):
-            src, dst = (elev, slot(me)) if kind else (ref_in, refbuf.at[me])
+            src, dst = (slot(me), slot(me)) if kind else (ref_in, refbuf.at[me])
             sent.append(remote(src, dst, send_sem, number, kind, me, peer))
             sent[-1].start()
     for kind in (1, 0):
@@ -125,10 +136,13 @@
             copy.start()
             sent.append(copy)
     others = [partner] + [flipped(source, 1) for source in sources]
-    for copy in local:
+    for copy in local[:1] + local[2:]:
         copy.wait()
+    for device in [me] + sources:
+        decode(device)
     for source in others:
         remote(slot(source), slot(source), send_sem, 0, 1, source, partner).wait_recv()
+        decode(source)
 
     lane = lax.broadcasted_iota(jnp.int32, (SUBLANES, LANES), 1)
     sublane = lax.broadcasted_iota(jnp.int32, (SUBLANES, LANES), 0)
@@ -162,7 +176,7 @@
             heights[
                 pl.ds(pl.multiple_of(step * SUBLANES, SUBLANES), SUBLANES),
                 group * LANES : (group + 1) * LANES,
-            ] = total * (1.0 / 256.0)
+            ] = total * (HEIGHT_REACH / HEIGHT_STEPS / 256.0)
         return carry
 
     lax.fori_loop(0, rows // SUBLANES, eight_rows, 0)
@@ -299,6 +313,8 @@
         out_specs=pl.BlockSpec(memory_space=pltpu.VMEM),
         scratch_shapes=[
             pltpu.VMEM((n * elevation_tiles.shape[0],) + elevation_tiles.shape[1:], jnp.float32),
+            pltpu.VMEM(elevation_tiles.shape, jnp.float32),
+            pltpu.VMEM((n, elevation_tiles.shape[0] * SUBLANES, cols), jnp.int16),
             pltpu.VMEM((n, 2, lines, line), jnp.bfloat16),
             pltpu.VMEM((2, n * lines, line), jnp.float32),
             pltpu.VMEM((rows, cols), jnp.float32),

time: 14.8 us -> 13.4 us (0.905); the launches traced: 14.7 us -> 13.1 us
  Pallas kernels: 14.1 us -> 12.5 us
    pallas_call x1, Pallas kernels: 14.1 us -> 12.5 us  [per_device(): pl.pallas_call(functools.partial(kernel, n), out_shape=pltpu.VMEM(seconda...]
where the time goes in v3:
time: 13.4 us; the launch traced here: 13.1 us
  Pallas kernels  12.5 us (93%)
  local copies, waits for them, and re-layouts  0.62 us (5%)
    pallas_call x1, Pallas kernels, per_device(): pl.pallas_call(functools.partial(kernel, n), out_shape=pltpu.VMEM(seconda...  12.5 us
    unnamed x1, local copies, waits for them, and re-layouts  0.62 us

profile of v3, /device:TPU:1, one launch (start us, length us, event | category | flops | bytes accessed | tf_op | source)
XLA Modules:
  0.0 13.1 jit_solution(15325740518912729453)
XLA Ops:
  0.0 12.5 %shard_map.127 = bf16[1,2,32,256]{3,2,1,0:T(8,128)(2,1)S(1)} custom-call(f32[2,8,256]{2,1,0:T(8,128)} %elev.1, bf16[2,8,64]{2,1,0:T(8,128)(2,1)} %ref_in.1, bf16[1,2,32,256]{3,2,1,0:T(8,128)(2,1)} %sec.1, f32[1,2]{1,0:T(1,128)} %base_h.1, s32[128]{0:T(128)} %bitcast.3, s32[128]{0:T(128)} %row_h.1, s32[128]{0:T(128)} %col_h.1, s32[2,128]{1,0:T(2,128)} %bitcast.2, ...), custom_call_target="tpu_custom_call" | custom-call | tf_op jit(solution)/shard_map/pallas_call | solution.py:309
  12.5 0.6 %copy.15 = bf16[1,2,32,256]{3,2,1,0:T(8,128)(2,1)} copy(bf16[1,2,32,256]{3,2,1,0:T(8,128)(2,1)S(1)} %shard_map.127) | data formatting | bytes 65536

commit v4 on v3

--- a/solution.py
+++ b/solution.py
@@ -85,9 +85,12 @@
         return codes.at[device]
 
     def decode(device):
-        tiles[pl.ds(device * own, own)] = (
-            codes[device].astype(jnp.int32).astype(jnp.float32).reshape(elev.shape)
-        )
+        whole = codes[device].astype(jnp.int32).astype(jnp.float32)
+        start = pl.multiple_of(SUBLANES + device * whole.shape[0], SUBLANES)
+        for group in range(cols // LANES):
+            tiles[group, pl.ds(start, whole.shape[0]), :] = whole[
+                :, group * LANES : (group + 1) * LANES
+            ]
 
     local = [
         pltpu.make_async_copy(ref_in, refbuf.at[me], local_sem.at[0]),
@@ -135,11 +138,12 @@
             copy.wait_recv()
             copy.start()
             sent.append(copy)
+        if kind:
+            for device in [me] + sources:
+                decode(device)
     others = [partner] + [flipped(source, 1) for source in sources]
     for copy in local[:1] + local[2:]:
         copy.wait()
-    for device in [me] + sources:
-        decode(device)
     for source in others:
         remote(slot(source), slot(source), send_sem, 0, 1, source, partner).wait_recv()
         decode(source)
@@ -159,13 +163,13 @@
                     tile, col = first_tile[b], first_col[b]
                     fy = frac[0, b].astype(jnp.float32)
                     fx = frac[1, b].astype(jnp.float32)
-                    near = tiles[tile, :, 0:LANES]
+                    top = (tile + 1) * SUBLANES + first_row[b] - band * BLOCK_LINES
+                    upper = tiles[0, pl.ds(top, SUBLANES), :]
+                    lower = tiles[0, pl.ds(top + 1, SUBLANES), :]
                     for other in range(1, cols // LANES):
-                        far = tiles[tile, :, other * LANES : (other + 1) * LANES]
-                        near = jnp.where(lane + (other - 1) * LANES >= col, near, far)
-                    move = band * BLOCK_LINES + SUBLANES - first_row[b]
-                    upper = pltpu.roll(near, (move) & (SUBLANES - 1), 0)
-                    lower = pltpu.roll(near, (move - 1) & (SUBLANES - 1), 0)
+                        near = lane + (other - 1) * LANES >= col
+                        upper = jnp.where(near, upper, tiles[other, pl.ds(top, SUBLANES), :])
+                        lower = jnp.where(near, lower, tiles[other, pl.ds(top + 1, SUBLANES), :])
                     mixed = 16.0 * upper + fy * (lower - upper)
                     shift = place * BLOCK_SAMPLES + cols - col
                     left = pltpu.roll(mixed, (shift) & (LANES - 1), 1)
@@ -179,7 +183,7 @@
             ] = total * (HEIGHT_REACH / HEIGHT_STEPS / 256.0)
         return carry
 
-    lax.fori_loop(0, rows // SUBLANES, eight_rows, 0)
+    lax.fori_loop(0, rows // SUBLANES, eight_rows, 0, unroll=True)
 
     for source in others:
         remote(refbuf.at[source], refbuf.at[source], send_sem, 0, 0, source, partner).wait_recv()
@@ -312,7 +316,9 @@
         in_specs=[anywhere] * 13,
         out_specs=pl.BlockSpec(memory_space=pltpu.VMEM),
         scratch_shapes=[
-            pltpu.VMEM((n * elevation_tiles.shape[0],) + elevation_tiles.shape[1:], jnp.float32),
+            pltpu.VMEM(
+                (cols // LANES, (n * elevation_tiles.shape[0] + 2) * SUBLANES, LANES), jnp.float32
+            ),
             pltpu.VMEM(elevation_tiles.shape, jnp.float32),
             pltpu.VMEM((n, elevation_tiles.shape[0] * SUBLANES, cols), jnp.int16),
             pltpu.VMEM((n, 2, lines, line), jnp.bfloat16),

time: 13.4 us -> 12.9 us (0.963)
  Pallas kernels: 12.5 us -> 12 us
    pallas_call x1, Pallas kernels: 12.5 us -> 12 us  [per_device(): pl.pallas_call(functools.partial(kernel, n), out_shape=pltpu.VMEM(seconda...]
where the time goes in v4:
time: 12.9 us; the launch traced here: 12.7 us
  Pallas kernels  12 us (93%)
  local copies, waits for them, and re-layouts  0.62 us (5%)
    pallas_call x1, Pallas kernels, per_device(): pl.pallas_call(functools.partial(kernel, n), out_shape=pltpu.VMEM(seconda...  12 us
    unnamed x1, local copies, waits for them, and re-layouts  0.62 us

profile of v4, /device:TPU:1, one launch (start us, length us, event | category | flops | bytes accessed | tf_op | source)
XLA Modules:
  0.0 12.7 jit_solution(4748487087495958714)
XLA Ops:
  0.0 12.0 %shard_map.127 = bf16[1,2,32,256]{3,2,1,0:T(8,128)(2,1)S(1)} custom-call(f32[2,8,256]{2,1,0:T(8,128)} %elev.1, bf16[2,8,64]{2,1,0:T(8,128)(2,1)} %ref_in.1, bf16[1,2,32,256]{3,2,1,0:T(8,128)(2,1)} %sec.1, f32[1,2]{1,0:T(1,128)} %base_h.1, s32[128]{0:T(128)} %bitcast.3, s32[128]{0:T(128)} %row_h.1, s32[128]{0:T(128)} %col_h.1, s32[2,128]{1,0:T(2,128)} %bitcast.2, ...), custom_call_target="tpu_custom_call" | custom-call | tf_op jit(solution)/shard_map/pallas_call | solution.py:313
  12.1 0.6 %copy.15 = bf16[1,2,32,256]{3,2,1,0:T(8,128)(2,1)} copy(bf16[1,2,32,256]{3,2,1,0:T(8,128)(2,1)S(1)} %shard_map.127) | data formatting | bytes 65536

commit v5 on v4

--- a/solution.py
+++ b/solution.py
@@ -75,6 +75,8 @@
     partner = flipped(me, 1)
     peers = [flipped(me, 2 * k) for k in reversed(range(1, n // 2))]
     sources = peers[::-1]
+    elev_copy = pltpu.make_async_copy(elev, elevbuf, local_sem.at[1])
+    elev_copy.start()
     barrier = pltpu.get_barrier_semaphore()
     for peer in peers + [partner]:
         pl.semaphore_signal(
@@ -94,7 +96,7 @@
 
     local = [
         pltpu.make_async_copy(ref_in, refbuf.at[me], local_sem.at[0]),
-        pltpu.make_async_copy(elev, elevbuf, local_sem.at[1]),
+        elev_copy,
         pltpu.make_async_copy(sec, secbuf, local_sem.at[2]),
         pltpu.make_async_copy(into_h, into, local_sem.at[3]),
         pltpu.make_async_copy(down_h, down, local_sem.at[4]),
@@ -107,8 +109,7 @@
         pltpu.make_async_copy(col_h, first_col, local_sem.at[11]),
         pltpu.make_async_copy(frac_h, frac, local_sem.at[12]),
     ]
-    local[1].start()
-    for copy in local[8:] + local[:1] + local[2:8]:
+    for copy in local[:1]:
         copy.start()
 
     def remote(src, dst, sends, number, kind, source, device):
@@ -131,6 +132,8 @@
             src, dst = (slot(me), slot(me)) if kind else (ref_in, refbuf.at[me])
             sent.append(remote(src, dst, send_sem, number, kind, me, peer))
             sent[-1].start()
+    for copy in local[8:] + local[2:8]:
+        copy.start()
     for kind in (1, 0):
         for number, source in enumerate(sources):
             where = slot(source) if kind else refbuf.at[source]

time: 12.9 us -> 12.9 us (level)
  no operation moved by 1% of the time
where the time goes in v5:
time: 12.9 us; the launch traced here: 12.7 us
  Pallas kernels  12 us (93%)
  local copies, waits for them, and re-layouts  0.62 us (5%)
    pallas_call x1, Pallas kernels, per_device(): pl.pallas_call(functools.partial(kernel, n), out_shape=pltpu.VMEM(seconda...  12 us
    unnamed x1, local copies, waits for them, and re-layouts  0.62 us

profile of v5, /device:TPU:1, one launch (start us, length us, event | category | flops | bytes accessed | tf_op | source)
XLA Modules:
  0.0 12.7 jit_solution(9543857475668158646)
XLA Ops:
  0.0 12.0 %shard_map.127 = bf16[1,2,32,256]{3,2,1,0:T(8,128)(2,1)S(1)} custom-call(f32[2,8,256]{2,1,0:T(8,128)} %elev.1, bf16[2,8,64]{2,1,0:T(8,128)(2,1)} %ref_in.1, bf16[1,2,32,256]{3,2,1,0:T(8,128)(2,1)} %sec.1, f32[1,2]{1,0:T(1,128)} %base_h.1, s32[128]{0:T(128)} %bitcast.3, s32[128]{0:T(128)} %row_h.1, s32[128]{0:T(128)} %col_h.1, s32[2,128]{1,0:T(2,128)} %bitcast.2, ...), custom_call_target="tpu_custom_call" | custom-call | tf_op jit(solution)/shard_map/pallas_call | solution.py:316
  12.1 0.6 %copy.15 = bf16[1,2,32,256]{3,2,1,0:T(8,128)(2,1)} copy(bf16[1,2,32,256]{3,2,1,0:T(8,128)(2,1)S(1)} %shard_map.127) | data formatting | bytes 65536
